TPU v7x, 256 devices: a whole 4x4x8 slice. The times are simulated.
256 devices in a mesh: section: 2 (over x_hi), lat: 4 (over x_lo, core), lon: 32 (over y, z).
Axes of the slice: x: 4 (x_hi: 2, x_lo: 2; x = x_hi * 2 + x_lo), y: 4, z: 8, core: 2. Of those that a mesh axis runs over, the one named last changes fastest.
Arguments:
- window_input: bfloat16 [2, 16, 2176, 256], P(None, 'lat', 'lon'), may hold values from -8 to 8
- output_cotangent: bfloat16 [2, 16, 2176, 256], P(None, 'lat', 'lon'), may hold values from -6 to 6
- ocean_mask: int32 [16, 2176], P('lat', 'lon'), may hold values 0 or 1
- dw_kernel: bfloat16 [2, 49, 256], P('section'), may hold values from -1.5 to 1.5
- channel_params: bfloat16 [2, 5, 256], P('section'), may hold values from -1.5 to 1.5
- up_weight: bfloat16 [2, 256, 1024], P('section'), may hold values from -0.375 to 0.375
- up_bias: bfloat16 [2, 1024], P('section'), may hold values from -3 to 3
- down_weight: bfloat16 [2, 1024, 256], P('section'), may hold values from -0.1875 to 0.1875
Outputs:
- boundary: bfloat16 [2, 2, 16, 2176, 256], P('section', None, 'lat', 'lon')
- grad_kernel: float32 [2, 49, 256], P('section')
- grad_channels: float32 [2, 5, 256], P('section')
- grad_up: float32 [2, 256, 1024], P('section')
- grad_up_bias: float32 [2, 1024], P('section')
- grad_down: float32 [2, 1024, 256], P('section')
All inputs are finite; a program needn't handle non-finite values. No bound on the sum of `ocean_mask` on one device may be relied on, other than what follows from the above.
Results may differ from a plain program's by a relative error of at most 0.012.
Values may be sent and summed in bfloat16 or wider, within the bound.
A program may use at most 128 MiB of HBM per device.

v0:
```python
import math
import jax
import jax.numpy as jnp
from jax import lax
from jax.sharding import PartitionSpec as P

KERNEL = 7
ROWS_DEV = 4
COLS_DEV = 68
BATCH = 2
norm_eps = 1e-06
gelu_scale = 0.7978845608028654
gelu_cubic = 0.044715
rows_contract = (((0,), (0,)), ((), ()))
cols_contract = (((1,), (1,)), ((), ()))


def padded_2(block, sides, width, periodic):
    for axis, dim in sides:
        count = lax.axis_size(axis)
        forward = [(i, i + 1) for i in range(count - 1)]
        if periodic:
            forward.append((count - 1, 0))
        backward = [(target, source) for source, target in forward]
        low = lax.ppermute(
            lax.slice_in_dim(block, block.shape[dim] - width, None, axis=dim), axis, forward
        )
        high = lax.ppermute(lax.slice_in_dim(block, 0, width, axis=dim), axis, backward)
        block = jnp.concatenate([low, block, high], axis=dim)
    return block


def from_behind(value, axis, by):
    count = lax.axis_size(axis)
    pairs = [(i, i + by) for i in range(count) if 0 <= i + by < count]
    return lax.ppermute(value, axis, pairs)


def gelu_value(values):
    inner = gelu_scale * (values + gelu_cubic * values * values * values)
    return 0.5 * values * (1.0 + jnp.tanh(inner))


def gelu_slope(values):
    tangent = jnp.tanh(gelu_scale * (values + gelu_cubic * values * values * values))
    return 0.5 * (1.0 + tangent) + 0.5 * values * (1.0 - tangent * tangent) * gelu_scale * (
        1.0 + 3.0 * gelu_cubic * values * values
    )


def depthwise(padded, kernel, row_count, col_count):
    summed = jnp.zeros((padded.shape[0], row_count, col_count, padded.shape[3]), jnp.float32)
    for offset in range(KERNEL * KERNEL):
        row_off, col_off = divmod(offset, KERNEL)
        window = padded[:, row_off : row_off + row_count, col_off : col_off + col_count, :]
        summed = summed + window.astype(jnp.float32) * kernel[offset].astype(jnp.float32)
    return summed


def kernel_grads(padded, grad_conv, row_count, col_count):
    channels = grad_conv.shape[-1]
    grad_wide = grad_conv.astype(jnp.float32)
    tap_sums = []
    for offset in range(KERNEL * KERNEL):
        row_off, col_off = divmod(offset, KERNEL)
        window = padded[:, row_off : row_off + row_count, col_off : col_off + col_count, :].astype(
            jnp.float32
        )
        tap_sums.append(jnp.sum((grad_wide * window).reshape(-1, channels), axis=0))
    return (jnp.stack(tap_sums), jnp.sum(grad_wide.reshape(-1, channels), axis=0))


def cell_forward(conv_out, inputs, sea_mask, params, w_up, b_up, w_down):
    average = jnp.mean(conv_out, axis=-1, keepdims=True)
    centered = conv_out - average
    inverse = lax.rsqrt(jnp.mean(centered * centered, axis=-1, keepdims=True) + norm_eps)
    normed = centered * inverse
    scaled = (normed * params[1].astype(jnp.float32) + params[2].astype(jnp.float32)).astype(
        jnp.bfloat16
    )
    channels = scaled.shape[-1]
    flat_rows = scaled.reshape(-1, channels)
    hidden = jnp.dot(flat_rows, w_up, preferred_element_type=jnp.float32) + b_up.astype(jnp.float32)
    active = gelu_value(hidden).astype(jnp.bfloat16)
    branch = jnp.dot(active, w_down, preferred_element_type=jnp.float32) + params[3].astype(
        jnp.float32
    )
    branch = branch.reshape(conv_out.shape)
    output = (
        sea_mask * (inputs.astype(jnp.float32) + params[4].astype(jnp.float32) * branch)
    ).astype(jnp.bfloat16)
    return (output, (normed, inverse, flat_rows, hidden, active, branch))


def cell_backward(saved, sea_mask, cotangent, params, w_up, w_down):
    normed, inverse, flat_rows, hidden, active, branch = saved
    channels = normed.shape[-1]
    upstream = sea_mask * cotangent.astype(jnp.float32)
    grad_scale = jnp.sum((upstream * branch).reshape(-1, channels), axis=0)
    grad_branch = (
        (params[4].astype(jnp.float32) * upstream).astype(jnp.bfloat16).reshape(-1, channels)
    )
    grad_down = lax.dot_general(
        active, grad_branch, rows_contract, preferred_element_type=jnp.float32
    )
    grad_out_bias = jnp.sum(grad_branch.astype(jnp.float32), axis=0)
    grad_active = lax.dot_general(
        grad_branch, w_down, cols_contract, preferred_element_type=jnp.float32
    )
    grad_hidden = (grad_active * gelu_slope(hidden)).astype(jnp.bfloat16)
    grad_up = lax.dot_general(
        flat_rows, grad_hidden, rows_contract, preferred_element_type=jnp.float32
    )
    grad_up_bias = jnp.sum(grad_hidden.astype(jnp.float32), axis=0)
    grad_scaled = lax.dot_general(
        grad_hidden, w_up, cols_contract, preferred_element_type=jnp.float32
    )
    grad_scaled = grad_scaled.reshape(normed.shape)
    grad_gain = jnp.sum((grad_scaled * normed).reshape(-1, channels), axis=0)
    grad_shift = jnp.sum(grad_scaled.reshape(-1, channels), axis=0)
    grad_normed = grad_scaled * params[1].astype(jnp.float32)
    first_mean = jnp.mean(grad_normed, axis=-1, keepdims=True)
    second_mean = jnp.mean(grad_normed * normed, axis=-1, keepdims=True)
    grad_conv = (inverse * (grad_normed - first_mean - normed * second_mean)).astype(jnp.bfloat16)
    small = (grad_gain, grad_shift, grad_out_bias, grad_scale)
    return (grad_conv, upstream, small, grad_up, grad_up_bias, grad_down)


def halo_field(field):
    reach = KERNEL // 2
    beside_all = padded_2(field, (("lon", 2),), reach, True)
    return padded_2(beside_all, (("lat", 1),), reach, False)


def run_forward(field, sea_mask, weights):
    kernel, params, w_up, b_up, w_down = weights
    padded = halo_field(field)
    conv_out = depthwise(padded, kernel, field.shape[1], field.shape[2]) + params[0].astype(
        jnp.float32
    )
    output, saved = cell_forward(conv_out, field, sea_mask, params, w_up, b_up, w_down)
    return (output, (padded, saved))


def run_backward(stored, sea_mask, weights, cotangent):
    kernel, params, w_up, b_up, w_down = weights
    padded, saved = stored
    row_count, col_count = (cotangent.shape[1], cotangent.shape[2])
    grad_conv, upstream, small, grad_up, grad_bias, grad_down = cell_backward(
        saved, sea_mask, cotangent, params, w_up, w_down
    )
    tap_sums, bias_sum = kernel_grads(padded, grad_conv, row_count, col_count)
    spread = depthwise(halo_field(grad_conv), kernel[::-1], row_count, col_count)
    grad_input = (upstream + spread).astype(jnp.bfloat16)
    return (grad_input, (tap_sums, jnp.stack((bias_sum,) + small), grad_up, grad_bias, grad_down))


def on_device(
    window_input,
    output_cotangent,
    ocean_mask,
    dw_kernel,
    channel_params,
    up_weight,
    up_bias,
    down_weight,
):
    section = lax.axis_index("section")
    first_section = section == 0
    sea_mask = ocean_mask.astype(jnp.float32)[None, :, :, None]
    batch_size = window_input.shape[0]
    local = (dw_kernel[0], channel_params[0], up_weight[0], up_bias[0], down_weight[0])
    micro = 1
    size_micro = batch_size // micro
    zero_field = jnp.zeros((size_micro,) + window_input.shape[1:], jnp.bfloat16)
    received = zero_field
    stored = []
    outputs = []
    for tick in range(micro + 1):
        if tick < micro:
            own_part = window_input
        else:
            own_part = zero_field
        current = jnp.where(first_section, own_part, received)
        result, kept = run_forward(current, sea_mask, local)
        stored.append(kept)
        outputs.append(result)
        if tick < micro:
            received = from_behind(result, "section", 1)
    received = zero_field
    grad_inputs = []
    totals = None
    for tick in range(micro + 1):
        if tick < micro:
            own_part = output_cotangent
        else:
            own_part = zero_field
        current = jnp.where(first_section, received, own_part)
        kept = jax.tree.map(
            lambda before, behind: jnp.where(first_section, before, behind),
            stored[max(tick - 1, 0)],
            stored[min(tick + 1, micro)],
        )
        grad_input, grads = run_backward(kept, sea_mask, local, current)
        counted = jnp.where(
            first_section, 1.0 if tick >= 1 else 0.0, 1.0 if tick < micro else 0.0
        ).astype(jnp.float32)
        weighted = jax.tree.map(lambda member: member * counted, grads)
        if totals is None:
            totals = weighted
        else:
            totals = jax.tree.map(jnp.add, totals, weighted)
        grad_inputs.append(grad_input)
        if tick < micro:
            received = from_behind(grad_input, "section", -1)
    final = jnp.concatenate(outputs[1:], axis=0)
    starts = jnp.concatenate(grad_inputs[1:], axis=0)
    boundary = jnp.where(first_section, starts, final)[None]
    owned = tuple((member[None] for member in totals))
    summed = lax.psum((owned[0], owned[1], owned[2], owned[3], owned[4]), ("lat", "lon"))
    factor = 1.0 / math.sqrt(BATCH * ROWS_DEV * COLS_DEV)
    return (
        boundary,
        summed[0] * factor,
        summed[1] * factor,
        summed[2] * factor,
        summed[3] * factor,
        summed[4] * factor,
    )


def solution(mesh):
    in_specs = (
        P(None, "lat", "lon", None),
        P(None, "lat", "lon", None),
        P("lat", "lon"),
        P("section", None, None),
        P("section", None, None),
        P("section", None, None),
        P("section", None),
        P("section", None, None),
    )
    out_specs = (
        P("section", None, "lat", "lon", None),
        P("section", None, None),
        P("section", None, None),
        P("section", None, None),
        P("section", None),
        P("section", None, None),
    )
    return jax.shard_map(
        on_device, mesh=mesh, in_specs=in_specs, out_specs=out_specs, check_vma=False
    )
```

profile of v0, /device:TPU:4, one launch (start us, length us, event | category | flops | bytes accessed | tf_op | source)
XLA Modules:
  0.0 1807.4 jit_solution(11287534964740938511)
XLA Ops:
  8.4 8.4 collective-permute-start.1
  18.9 4.9 collective-permute-done
  28.0 2.1 collective-permute-done.3
  30.9 5.6 fusion.257
  38.1 3.1 fusion.4
  42.2 2.0 convolution_add_fusion.1
  48.2 8.8 collective-permute-done.4
  60.9 3.7 collective-permute-done.5
  65.6 3.9 collective-permute-start.7
  73.1 2.0 collective-permute-done.8
  76.1 5.6 fusion.255
  83.1 4.7 fusion.9
  91.4 2.2 multiply_reduce_fusion.3
  100.1 2.0 collective-permute-start.9
  103.8 3.3 collective-permute-done.9
  107.3 5.4 collective-permute-start.11
  117.4 4.7 add_convert_fusion.1
  127.7 2.0 multiply_reduce_fusion.2
  129.8 2.8 convert_reduce_fusion.2
  149.3 553.0 %all-reduce = (f32[1,49,256]{2,0,1:T(1,128)S(1)}, f32[1,5,256]{2,0,1:T(1,128)S(1)}, f32[1,1024]{1,0:T(1,128)S(1)}) all-reduce(f32[1,49,256]{2,0,1:T(1,128)S(1)} %multiply_add_fusion.3, f32[1,5,256]{2,0,1:T(1,128)S(1)} %multiply_add_fusion.4, f32[1,1024]{1,0:T(1,128)S(1)} %bitcast.416), channel_id=1, replica_groups=mesh['section'=2,'lat'=4,'lon'=32] {'lat','lon'}, use_global_device_ids=true, to_apply=%region_106.107 | all-reduce | flops 14848 | bytes 118784 | tf_op jit(solution)/shard_map/psum | solution.py:220
  707.4 4.9 collective-permute-done.17
  712.8 5.5 fusion.252
  719.1 1078.0 %all-reduce.4.cloned.1.call-done = (f32[1,256,1024]{2,1,0:T(8,128)}, f32[1,1024,256]{2,1,0:T(8,128)}) async-done(((f32[1,256,1024]{2,1,0:T(8,128)}, f32[1,1024,256]{2,1,0:T(8,128)}), (f32[1,256,1024]{2,1,0:T(8,128)}, f32[1,1024,256]{2,1,0:T(8,128)})) %all-reduce.4.cloned.1.call-update) | async-done | bytes 2097168 | tf_op jit(solution)/shard_map/psum | solution.py:220
  1797.0 2.4 broadcast_multiply_fusion.1
  (578 shorter events, 68.9 us)
Async XLA Ops:
  7.2 31.0 %copy-start = (bf16[1,256,1024]{2,1,0:T(8,128)(2,1)S(1)}, bf16[1,256,1024]{2,1,0:T(8,128)(2,1)}, u32[]{:S(2)}) copy-start(bf16[1,256,1024]{2,1,0:T(8,128)(2,1)} %param.13) | copy-start | bytes 1572868
  7.2 1789.8 %all-reduce.4.cloned.1.call-start = ((), (), s32[]{:S(2)}) async-start(), calls=%async_computation | async-start | bytes 4194304 | tf_op jit(solution)/shard_map/psum | solution.py:220
  8.4 10.5 collective-permute-start.1
  16.8 7.1 collective-permute-start
  17.8 58.0 %copy-start.33 = (f32[1,1,256]{2,1,0:T(1,128)}, f32[1,1,256]{2,1,0:T(1,128)S(1)}, u32[]{:S(2)}) copy-start(f32[1,1,256]{2,1,0:T(1,128)S(1)} %get-tuple-element.177) | copy-start | bytes 3076
  17.8 58.0 %copy-start.35 = (f32[1,1,256]{2,1,0:T(1,128)}, f32[1,1,256]{2,1,0:T(1,128)S(1)}, u32[]{:S(2)}) copy-start(f32[1,1,256]{2,1,0:T(1,128)S(1)} %get-tuple-element.178) | copy-start | bytes 3076
  17.8 58.0 %copy-start.37 = (f32[1,1,256]{2,1,0:T(1,128)}, f32[1,1,256]{2,1,0:T(1,128)S(1)}, u32[]{:S(2)}) copy-start(f32[1,1,256]{2,1,0:T(1,128)S(1)} %get-tuple-element.179) | copy-start | bytes 3076
  24.0 4.0 collective-permute-start.2
  25.3 4.8 collective-permute-start.3
  45.3 36.4 %copy-start.4 = (f32[2,4,68,256]{3,2,1,0:T(8,128)}, f32[2,4,68,256]{3,2,1,0:T(8,128)S(1)}, u32[]{:S(2)}) copy-start(f32[2,4,68,256]{3,2,1,0:T(8,128)S(1)} %reshape.2385) | copy-start | bytes 1671172
  47.0 10.1 collective-permute-start.4
  57.1 3.8 collective-permute-start.6
  57.6 7.1 collective-permute-start.5
  65.6 7.5 collective-permute-start.7
  69.6 5.5 collective-permute-start.8
  100.1 3.7 collective-permute-start.10
  100.1 7.1 collective-permute-start.9
  107.3 9.2 collective-permute-start.11
  112.7 4.0 collective-permute-start.12
  122.2 5.5 collective-permute-start.13
  143.0 559.9 %collective-permute-start.15 = (bf16[2,4,3,256]{3,2,1,0:T(4,128)(2,1)S(1)}, bf16[2,4,3,256]{3,2,1,0:T(4,128)(2,1)S(1)}, u32[]{:S(2)}, u32[]{:S(2)}) collective-permute-start(bf16[2,4,3,256]{3,2,1,0:T(4,128)(2,1)S(1)} %get-tuple-element.158), channel_id=1, source_target_pairs={{1,0},{2,1},{3,2},{4,3},{5,4},{6,5},{7,6},{8,7},{9,8},{10,9},{11,1... | collective-permute-start | bytes 36872 | tf_op jit(solution)/shard_map/ppermute | solution.py:28
  143.4 559.5 %collective-permute-start.14 = (bf16[2,4,3,256]{3,2,1,0:T(4,128)(2,1)S(1)}, bf16[2,4,3,256]{3,2,1,0:T(4,128)(2,1)S(1)}, u32[]{:S(2)}, u32[]{:S(2)}) collective-permute-start(bf16[2,4,3,256]{3,2,1,0:T(4,128)(2,1)S(1)} %get-tuple-element.157), channel_id=1, source_target_pairs={{0,1},{1,2},{2,3},{3,4},{4,5},{5,6},{6,7},{7,8},{8,9},{9,10},{10,1... | collective-permute-start | bytes 36872 | tf_op jit(solution)/shard_map/ppermute | solution.py:25
  703.4 4.0 collective-permute-start.16
  704.8 7.5 collective-permute-start.17
  (182 other events, 971.4 us)
Sparse Core Ops, SparseCore 0:
  703.0 1093.9 all-reduce.3
where the time goes:
time: 1810 us
  waiting for transfers between devices  1110 us (61%)
  blocking collectives  553 us (31%)
  other arithmetic  51.6 us (3%)
  starting transfers between devices  34.9 us (2%)
  matrix products  23.5 us (1%)
    psum x1, waiting for transfers between devices, on_device(): lax.psum((owned[0], owned[1], owned[2], owned[3], owned[4]), ('lat', 'lon'))  1080 us
    psum x1, blocking collectives, on_device(): lax.psum((owned[0], owned[1], owned[2], owned[3], owned[4]), ('lat', 'lon'))  553 us
  transfers between devices with their start and end apart: 19, of which 12 were waited for; matrix products, arithmetic and copies ran while one was open for 1% of the time, Pallas kernels for 0%

commit v1 on v0

--- a/solution.py
+++ b/solution.py
@@ -217,7 +217,8 @@
     starts = jnp.concatenate(grad_inputs[1:], axis=0)
     boundary = jnp.where(first_section, starts, final)[None]
     owned = tuple((member[None] for member in totals))
-    summed = lax.psum((owned[0], owned[1], owned[2], owned[3], owned[4]), ("lat", "lon"))
+    one_axis = lax.psum((owned[0], owned[1], owned[2], owned[3], owned[4]), "lon")
+    summed = lax.psum(one_axis, "lat")
     factor = 1.0 / math.sqrt(BATCH * ROWS_DEV * COLS_DEV)
     return (
         boundary,

time: 1810 us -> 372 us (0.21)
  waiting for transfers between devices: 1110 us -> 79.7 us
  blocking collectives: 553 us -> 155 us
    psum x1 -> x2, waiting for transfers between devices: 1080 us -> 47.9 us  [the longest x1 47.8 us: on_device(): summed = lax.psum(one_axis, 'lat')]
    psum x1 -> x2, blocking collectives: 553 us -> 155 us  [the longest x1 141 us: on_device(): lax.psum((owned[0], owned[1], owned[2], owned[3], owned[4]), 'lon')]
  transfers between devices with their start and end apart: 19 -> 20, of which waited for: 12 -> 12; matrix products, arithmetic and copies ran while one was open for 1% -> 6% of each run, Pallas kernels for 0% -> 0%
where the time goes in v1:
time: 372 us; the launch traced here: 369 us
  blocking collectives  155 us (42%)
  waiting for transfers between devices  79.7 us (21%)
  other arithmetic  47.8 us (13%)
  starting transfers between devices  37.1 us (10%)
  matrix products  19.6 us (5%)
  between operations  16.5 us (4%)
  local copies, waits for them, and re-layouts  13.8 us (4%)
    psum x1, blocking collectives, on_device(): lax.psum((owned[0], owned[1], owned[2], owned[3], owned[4]), 'lon')  141 us
    psum x1, waiting for transfers between devices, on_device(): summed = lax.psum(one_axis, 'lat')  47.8 us
    ppermute x8, starting transfers between devices, padded_2(): lax.ppermute(lax.slice_in_dim(block, block.shape[dim] - width, None, axis...  19.2 us
    ppermute x8, starting transfers between devices, padded_2(): lax.ppermute(lax.slice_in_dim(block, 0, width, axis=dim), axis, backward)  14.4 us
    psum x1, blocking collectives, on_device(): summed = lax.psum(one_axis, 'lat')  13.4 us
    ppermute x8, waiting for transfers between devices, padded_2(): lax.ppermute(lax.slice_in_dim(block, block.shape[dim] - width, None, axis...  12 us
    ppermute x8, waiting for transfers between devices, padded_2(): lax.ppermute(lax.slice_in_dim(block, 0, width, axis=dim), axis, backward)  10.2 us
    reduce_sum x2, other arithmetic, cell_forward(): average = jnp.mean(conv_out, axis=-1, keepdims=True)  9.75 us
  transfers between devices with their start and end apart: 20, of which 12 were waited for; matrix products, arithmetic and copies ran while one was open for 6% of the time, Pallas kernels for 0%

profile of v1, /device:TPU:4, one launch (start us, length us, event | category | flops | bytes accessed | tf_op | source)
XLA Modules:
  0.0 369.3 jit_solution(6849069413259147806)
XLA Ops:
  8.4 8.4 %collective-permute-start.1 = (bf16[2,4,3,256]{3,2,1,0:T(4,128)(2,1)S(1)}, bf16[2,4,3,256]{3,2,1,0:T(4,128)(2,1)S(1)}, u32[]{:S(2)}, u32[]{:S(2)}) collective-permute-start(bf16[2,4,3,256]{3,2,1,0:T(4,128)(2,1)S(1)} %get-tuple-element.169), channel_id=1, source_target_pairs={{1,0},{2,1},{3,2},{4,3},{5,4},{6,5},{7,6},{8,7},{9,8},{10,9},{11,1... | collective-permute-start | bytes 36872 | tf_op jit(solution)/shard_map/ppermute | solution.py:28
  18.7 5.1 %collective-permute-done = bf16[2,4,3,256]{3,2,1,0:T(4,128)(2,1)S(1)} collective-permute-done((bf16[2,4,3,256]{3,2,1,0:T(4,128)(2,1)S(1)}, bf16[2,4,3,256]{3,2,1,0:T(4,128)(2,1)S(1)}, u32[]{:S(2)}, u32[]{:S(2)}) %collective-permute-start) | collective-permute-done | bytes 12320 | tf_op jit(solution)/shard_map/ppermute | solution.py:25
  30.8 4.8 %fusion.257 = (f32[2,4,68]{2,1,0:T(4,128)S(1)}, f32[2,4,68,256]{3,2,1,0:T(8,128)S(1)}) fusion(f32[256]{0:T(256)S(1)} %bitcast.424, f32[256]{0:T(256)S(1)} %bitcast.332, bf16[2,7,74,256]{3,2,1,0:T(8,128)(2,1)S(1)} %get-tuple-element.157, f32[256]{0:T(256)S(1)} %bitcast.336, f32[256]{0:T(256)S(1)} %bitcast.224, f32[256]{0:T(256)S(1)} %bitcast.228, ...), kind=kLoop, calls=%fused_computation.622 | loop fusion | flops 23117280 | bytes 12611712 | tf_op jit(solution)/shard_map/reduce_sum | solution.py:74
  36.5 2.3 fusion.4
  42.4 8.8 %collective-permute-done.4 = bf16[2,4,68,256]{3,2,1,0:T(8,128)(2,1)S(1)} collective-permute-done((bf16[2,4,68,256]{3,2,1,0:T(8,128)(2,1)S(1)}, bf16[2,4,68,256]{3,2,1,0:T(8,128)(2,1)S(1)}, u32[]{:S(2)}, u32[]{:S(2)}) %collective-permute-start.4) | collective-permute-done | bytes 278560 | tf_op jit(solution)/shard_map/ppermute | solution.py:36
  55.1 3.6 collective-permute-done.5
  59.5 4.0 %collective-permute-start.7 = (bf16[2,3,74,256]{3,2,1,0:T(8,128)(2,1)}, bf16[2,3,74,256]{3,2,1,0:T(8,128)(2,1)S(1)}, u32[]{:S(2)}, u32[]{:S(2)}) collective-permute-start(bf16[2,3,74,256]{3,2,1,0:T(8,128)(2,1)} %get-tuple-element.154), channel_id=1, source_target_pairs={{0,32},{32,64},{64,96},{1,33},{33,65},{65,97},{2,34},{34,66},{66,9... | collective-permute-start | bytes 681992 | tf_op jit(solution)/shard_map/ppermute | solution.py:25
  66.0 2.8 collective-permute-done.8
  69.7 4.9 %fusion.255 = (f32[2,4,68]{2,1,0:T(4,128)S(1)}, f32[2,4,68,256]{3,2,1,0:T(8,128)S(1)}) fusion(f32[256]{0:T(256)S(1)} %bitcast.425, f32[256]{0:T(256)S(1)} %bitcast.333, bf16[2,7,74,256]{3,2,1,0:T(8,128)(2,1)S(1)} %get-tuple-element.153, f32[256]{0:T(256)S(1)} %bitcast.337, f32[256]{0:T(256)S(1)} %bitcast.225, f32[256]{0:T(256)S(1)} %bitcast.229, ...), kind=kLoop, calls=%fused_computation.621 | loop fusion | flops 23117280 | bytes 12611712 | tf_op jit(solution)/shard_map/reduce_sum | solution.py:74
  75.3 4.7 %fusion.9 = (f32[544,1024]{1,0:T(8,128)S(1)}, bf16[544,1024]{1,0:T(8,128)(2,1)}) fusion(f32[544,1024]{1,0:T(8,128)} %get-tuple-element.229, f32[1024]{0:T(1024)S(1)} %bitcast.533, pred[]{:T(512)S(6)} %eq.3, bf16[544,256]{1,0:T(8,128)(2,1)S(1)} %reshape.2387, bf16[1,256,1024]{2,1,0:T(8,128)(2,1)S(1)} %copy-done), kind=kOutput, calls=%fused_computation.115 | convolution fusion | flops 301367296 | bytes 6377473 | tf_op jit(solution)/shard_map/dot_general | solution.py:83
  83.4 2.2 multiply_reduce_fusion.3
  96.0 3.3 collective-permute-done.9
  99.5 5.4 %collective-permute-start.11 = (bf16[2,3,74,256]{3,2,1,0:T(8,128)(2,1)S(1)}, bf16[2,3,74,256]{3,2,1,0:T(8,128)(2,1)S(1)}, u32[]{:S(2)}, u32[]{:S(2)}) collective-permute-start(bf16[2,3,74,256]{3,2,1,0:T(8,128)(2,1)S(1)} %get-tuple-element.150), channel_id=1, source_target_pairs={{0,32},{32,64},{64,96},{1,33},{33,65},{65,97},{2,34},{34,66},{66,9... | collective-permute-start | bytes 681992 | tf_op jit(solution)/shard_map/ppermute | solution.py:25
  109.1 5.4 %add_convert_fusion.1 = bf16[2,4,68,256]{3,2,1,0:T(8,128)(2,1)} fusion(bf16[2,4,68,256]{3,2,1,0:T(8,128)(2,1)S(1)} %get-tuple-element.135, bf16[2,4,3,256]{3,2,1,0:T(4,128)(2,1)S(1)} %collective-permute-done.10, bf16[2,4,3,256]{3,2,1,0:T(4,128)(2,1)S(1)} %collective-permute-done.9, bf16[2,7,74,256]{3,2,1,0:T(8,128)(2,1)S(1)} %get-tuple-element.149, ...), kind=kLoop, calls=%fused_computation.354 | loop fusion | flops 23535616 | bytes 12609601 | tf_op jit(solution)/shard_map/convert_element_type | solution.py:154
  114.5 2.1 collective-permute-start.13
  120.5 2.7 multiply_reduce_fusion.2
  124.2 2.8 convert_reduce_fusion.2
  141.6 141.5 %all-reduce = (f32[1,49,256]{2,0,1:T(1,128)S(1)}, f32[1,5,256]{2,0,1:T(1,128)S(1)}, f32[1,1024]{1,0:T(1,128)S(1)}) all-reduce(f32[1,49,256]{2,0,1:T(1,128)S(1)} %multiply_add_fusion.3, f32[1,5,256]{2,0,1:T(1,128)S(1)} %multiply_add_fusion.4, f32[1,1024]{1,0:T(1,128)S(1)} %bitcast.419), channel_id=1, replica_groups=mesh['section'=2,'lat'=4,'lon'=32] {'lon'}, use_global_device_ids=true, to_apply=%region_106.107 | all-reduce | flops 14848 | bytes 118784 | tf_op jit(solution)/shard_map/psum | solution.py:220
  283.1 13.4 %all-reduce.2 = (f32[1,49,256]{2,0,1:T(1,128)S(1)}, f32[1,5,256]{2,0,1:T(1,128)S(1)}, f32[1,1024]{1,0:T(1,128)S(1)}) all-reduce(f32[1,49,256]{2,0,1:T(1,128)S(1)} %get-tuple-element.123, f32[1,5,256]{2,0,1:T(1,128)S(1)} %get-tuple-element.124, ...), channel_id=1, replica_groups=mesh['section'=2,'lat'=4,'lon'=32] {'lat'}, use_global_device_ids=true, to_apply=%region_107.108 | all-reduce | flops 14848 | bytes 118784 | tf_op jit(solution)/shard_map/psum | solution.py:221
  297.6 2.7 collective-permute-start.16
  302.8 2.1 collective-permute-done.17
  305.3 4.9 %fusion.252 = bf16[1,2,4,68,256]{4,3,2,1,0:T(8,128)(2,1)S(1)} fusion(f32[2,4,68,256]{3,2,1,0:T(8,128)S(1)} %copy-done.9, f32[256]{0:T(256)S(1)} %bitcast.418, f32[4,68]{1,0:T(4,128)S(1)} %convert_element_type.1601, f32[256]{0:T(256)S(1)} %bitcast.223, bf16[2,7,74,256]{3,2,1,0:T(8,128)(2,1)S(1)} %get-tuple-element.145, f32[256]{0:T(256)S(1)} %bitcast.343, ...), kind=kLoop, calls=%fused_computation.427 | loop fusion | flops 24510464 | bytes 13446209 | tf_op jit(solution)/shard_map/broadcast_in_dim | solution.py:218
  311.1 47.8 %all-reduce.9.cloned.1.call-done = (f32[1,256,1024]{2,1,0:T(8,128)}, f32[1,1024,256]{2,1,0:T(8,128)}) async-done(((f32[1,256,1024]{2,1,0:T(8,128)}, f32[1,1024,256]{2,1,0:T(8,128)}), (f32[1,256,1024]{2,1,0:T(8,128)}, f32[1,1024,256]{2,1,0:T(8,128)})) %all-reduce.9.cloned.1.call-update) | async-done | bytes 2097168 | tf_op jit(solution)/shard_map/psum | solution.py:221
  358.9 2.4 broadcast_multiply_fusion.1
  (496 shorter events, 64.5 us)
Async XLA Ops:
  7.2 29.3 %copy-start = (bf16[1,256,1024]{2,1,0:T(8,128)(2,1)S(1)}, bf16[1,256,1024]{2,1,0:T(8,128)(2,1)}, u32[]{:S(2)}) copy-start(bf16[1,256,1024]{2,1,0:T(8,128)(2,1)} %param.13) | copy-start | bytes 1572868
  7.2 290.0 %all-reduce.7.cloned.1.call-start = ((), (), s32[]{:S(2)}) async-start(), calls=%async_computation | async-start | bytes 4194304 | tf_op jit(solution)/shard_map/psum | solution.py:220
  8.4 10.3 %collective-permute-start.1 = (bf16[2,4,3,256]{3,2,1,0:T(4,128)(2,1)S(1)}, bf16[2,4,3,256]{3,2,1,0:T(4,128)(2,1)S(1)}, u32[]{:S(2)}, u32[]{:S(2)}) collective-permute-start(bf16[2,4,3,256]{3,2,1,0:T(4,128)(2,1)S(1)} %get-tuple-element.169), channel_id=1, source_target_pairs={{1,0},{2,1},{3,2},{4,3},{5,4},{6,5},{7,6},{8,7},{9,8},{10,9},{11,1... | collective-permute-start | bytes 36872 | tf_op jit(solution)/shard_map/ppermute | solution.py:28
  16.8 7.1 %collective-permute-start = (bf16[2,4,3,256]{3,2,1,0:T(4,128)(2,1)S(1)}, bf16[2,4,3,256]{3,2,1,0:T(4,128)(2,1)S(1)}, u32[]{:S(2)}, u32[]{:S(2)}) collective-permute-start(bf16[2,4,3,256]{3,2,1,0:T(4,128)(2,1)S(1)} %get-tuple-element.168), channel_id=1, source_target_pairs={{0,1},{1,2},{2,3},{3,4},{4,5},{5,6},{6,7},{7,8},{8,9},{9,10},{10,1... | collective-permute-start | bytes 36872 | tf_op jit(solution)/shard_map/ppermute | solution.py:25
  18.7 50.7 %copy-start.38 = (f32[1,1,256]{2,1,0:T(1,128)}, f32[1,1,256]{2,1,0:T(1,128)S(1)}, u32[]{:S(2)}) copy-start(f32[1,1,256]{2,1,0:T(1,128)S(1)} %get-tuple-element.217) | copy-start | bytes 3076
  18.7 50.7 %copy-start.41 = (f32[1,1,256]{2,1,0:T(1,128)}, f32[1,1,256]{2,1,0:T(1,128)S(1)}, u32[]{:S(2)}) copy-start(f32[1,1,256]{2,1,0:T(1,128)S(1)} %get-tuple-element.218) | copy-start | bytes 3076
  24.0 4.0 %collective-permute-start.2 = (bf16[2,3,74,256]{3,2,1,0:T(8,128)(2,1)S(1)}, bf16[2,3,74,256]{3,2,1,0:T(8,128)(2,1)S(1)}, u32[]{:S(2)}, u32[]{:S(2)}) collective-permute-start(bf16[2,3,74,256]{3,2,1,0:T(8,128)(2,1)S(1)} %get-tuple-element.158), channel_id=1, source_target_pairs={{0,32},{32,64},{64,96},{1,33},{33,65},{65,97},{2,34},{34,66},{66,9... | collective-permute-start | bytes 681992 | tf_op jit(solution)/shard_map/ppermute | solution.py:25
  25.3 4.8 %collective-permute-start.3 = (bf16[2,3,74,256]{3,2,1,0:T(8,128)(2,1)S(1)}, bf16[2,3,74,256]{3,2,1,0:T(8,128)(2,1)S(1)}, u32[]{:S(2)}, u32[]{:S(2)}) collective-permute-start(bf16[2,3,74,256]{3,2,1,0:T(8,128)(2,1)S(1)} %get-tuple-element.159), channel_id=1, source_target_pairs={{32,0},{64,32},{96,64},{33,1},{65,33},{97,65},{34,2},{66,34},{98,6... | collective-permute-start | bytes 681992 | tf_op jit(solution)/shard_map/ppermute | solution.py:28
  28.0 41.5 %copy-start.44 = (f32[1,1,256]{2,1,0:T(1,128)}, f32[1,1,256]{2,1,0:T(1,128)S(1)}, u32[]{:S(2)}) copy-start(f32[1,1,256]{2,1,0:T(1,128)S(1)} %get-tuple-element.189) | copy-start | bytes 3076
  41.1 10.1 %collective-permute-start.4 = (bf16[2,4,68,256]{3,2,1,0:T(8,128)(2,1)S(1)}, bf16[2,4,68,256]{3,2,1,0:T(8,128)(2,1)S(1)}, u32[]{:S(2)}, u32[]{:S(2)}) collective-permute-start(bf16[2,4,68,256]{3,2,1,0:T(8,128)(2,1)S(1)} %get-tuple-element.227), channel_id=1, source_target_pairs={{0,128},{1,129},{2,130},{3,131},{4,132},{5,133},{6,134},{7,135},{8... | collective-permute-start | bytes 835592 | tf_op jit(solution)/shard_map/ppermute | solution.py:36
  51.3 3.8 %collective-permute-start.6 = (bf16[2,4,3,256]{3,2,1,0:T(4,128)(2,1)S(1)}, bf16[2,4,3,256]{3,2,1,0:T(4,128)(2,1)S(1)}, u32[]{:S(2)}, u32[]{:S(2)}) collective-permute-start(bf16[2,4,3,256]{3,2,1,0:T(4,128)(2,1)S(1)} %get-tuple-element.167), channel_id=1, source_target_pairs={{1,0},{2,1},{3,2},{4,3},{5,4},{6,5},{7,6},{8,7},{9,8},{10,9},{11,1... | collective-permute-start | bytes 36872 | tf_op jit(solution)/shard_map/ppermute | solution.py:28
  51.6 7.1 %collective-permute-start.5 = (bf16[2,4,3,256]{3,2,1,0:T(4,128)(2,1)S(1)}, bf16[2,4,3,256]{3,2,1,0:T(4,128)(2,1)S(1)}, u32[]{:S(2)}, u32[]{:S(2)}) collective-permute-start(bf16[2,4,3,256]{3,2,1,0:T(4,128)(2,1)S(1)} %get-tuple-element.166), channel_id=1, source_target_pairs={{0,1},{1,2},{2,3},{3,4},{4,5},{5,6},{6,7},{7,8},{8,9},{9,10},{10,1... | collective-permute-start | bytes 36872 | tf_op jit(solution)/shard_map/ppermute | solution.py:25
  59.5 6.5 %collective-permute-start.7 = (bf16[2,3,74,256]{3,2,1,0:T(8,128)(2,1)}, bf16[2,3,74,256]{3,2,1,0:T(8,128)(2,1)S(1)}, u32[]{:S(2)}, u32[]{:S(2)}) collective-permute-start(bf16[2,3,74,256]{3,2,1,0:T(8,128)(2,1)} %get-tuple-element.154), channel_id=1, source_target_pairs={{0,32},{32,64},{64,96},{1,33},{33,65},{65,97},{2,34},{34,66},{66,9... | collective-permute-start | bytes 681992 | tf_op jit(solution)/shard_map/ppermute | solution.py:25
  63.5 5.2 %collective-permute-start.8 = (bf16[2,3,74,256]{3,2,1,0:T(8,128)(2,1)S(1)}, bf16[2,3,74,256]{3,2,1,0:T(8,128)(2,1)S(1)}, u32[]{:S(2)}, u32[]{:S(2)}) collective-permute-start(bf16[2,3,74,256]{3,2,1,0:T(8,128)(2,1)S(1)} %get-tuple-element.155), channel_id=1, source_target_pairs={{32,0},{64,32},{96,64},{33,1},{65,33},{97,65},{34,2},{66,34},{98,6... | collective-permute-start | bytes 681992 | tf_op jit(solution)/shard_map/ppermute | solution.py:28
  92.3 3.7 %collective-permute-start.10 = (bf16[2,4,3,256]{3,2,1,0:T(4,128)(2,1)S(1)}, bf16[2,4,3,256]{3,2,1,0:T(4,128)(2,1)S(1)}, u32[]{:S(2)}, u32[]{:S(2)}) collective-permute-start(bf16[2,4,3,256]{3,2,1,0:T(4,128)(2,1)S(1)} %get-tuple-element.165), channel_id=1, source_target_pairs={{1,0},{2,1},{3,2},{4,3},{5,4},{6,5},{7,6},{8,7},{9,8},{10,9},{11,1... | collective-permute-start | bytes 36872 | tf_op jit(solution)/shard_map/ppermute | solution.py:28
  92.3 7.1 %collective-permute-start.9 = (bf16[2,4,3,256]{3,2,1,0:T(4,128)(2,1)S(1)}, bf16[2,4,3,256]{3,2,1,0:T(4,128)(2,1)S(1)}, u32[]{:S(2)}, u32[]{:S(2)}) collective-permute-start(bf16[2,4,3,256]{3,2,1,0:T(4,128)(2,1)S(1)} %get-tuple-element.164), channel_id=1, source_target_pairs={{0,1},{1,2},{2,3},{3,4},{4,5},{5,6},{6,7},{7,8},{8,9},{9,10},{10,1... | collective-permute-start | bytes 36872 | tf_op jit(solution)/shard_map/ppermute | solution.py:25
  99.5 8.4 %collective-permute-start.11 = (bf16[2,3,74,256]{3,2,1,0:T(8,128)(2,1)S(1)}, bf16[2,3,74,256]{3,2,1,0:T(8,128)(2,1)S(1)}, u32[]{:S(2)}, u32[]{:S(2)}) collective-permute-start(bf16[2,3,74,256]{3,2,1,0:T(8,128)(2,1)S(1)} %get-tuple-element.150), channel_id=1, source_target_pairs={{0,32},{32,64},{64,96},{1,33},{33,65},{65,97},{2,34},{34,66},{66,9... | collective-permute-start | bytes 681992 | tf_op jit(solution)/shard_map/ppermute | solution.py:25
  104.9 3.9 %collective-permute-start.12 = (bf16[2,3,74,256]{3,2,1,0:T(8,128)(2,1)S(1)}, bf16[2,3,74,256]{3,2,1,0:T(8,128)(2,1)S(1)}, u32[]{:S(2)}, u32[]{:S(2)}) collective-permute-start(bf16[2,3,74,256]{3,2,1,0:T(8,128)(2,1)S(1)} %get-tuple-element.151), channel_id=1, source_target_pairs={{32,0},{64,32},{96,64},{33,1},{65,33},{97,65},{34,2},{66,34},{98,6... | collective-permute-start | bytes 681992 | tf_op jit(solution)/shard_map/ppermute | solution.py:28
  114.5 6.0 %collective-permute-start.13 = (bf16[2,4,68,256]{3,2,1,0:T(8,128)(2,1)}, bf16[2,4,68,256]{3,2,1,0:T(8,128)(2,1)}, u32[]{:S(2)}, u32[]{:S(2)}) collective-permute-start(bf16[2,4,68,256]{3,2,1,0:T(8,128)(2,1)} %add_convert_fusion.1), channel_id=1, source_target_pairs={{128,0},{129,1},{130,2},{131,3},{132,4},{133,5},{134,6},{135,7},{1... | collective-permute-start | bytes 835592 | tf_op jit(solution)/shard_map/ppermute | solution.py:36
  135.1 162.0 %collective-permute-start.15 = (bf16[2,4,3,256]{3,2,1,0:T(4,128)(2,1)S(1)}, bf16[2,4,3,256]{3,2,1,0:T(4,128)(2,1)S(1)}, u32[]{:S(2)}, u32[]{:S(2)}) collective-permute-start(bf16[2,4,3,256]{3,2,1,0:T(4,128)(2,1)S(1)} %get-tuple-element.163), channel_id=1, source_target_pairs={{1,0},{2,1},{3,2},{4,3},{5,4},{6,5},{7,6},{8,7},{9,8},{10,9},{11,1... | collective-permute-start | bytes 36872 | tf_op jit(solution)/shard_map/ppermute | solution.py:28
  135.2 161.9 %collective-permute-start.14 = (bf16[2,4,3,256]{3,2,1,0:T(4,128)(2,1)S(1)}, bf16[2,4,3,256]{3,2,1,0:T(4,128)(2,1)S(1)}, u32[]{:S(2)}, u32[]{:S(2)}) collective-permute-start(bf16[2,4,3,256]{3,2,1,0:T(4,128)(2,1)S(1)} %get-tuple-element.162), channel_id=1, source_target_pairs={{0,1},{1,2},{2,3},{3,4},{4,5},{5,6},{6,7},{7,8},{8,9},{9,10},{10,1... | collective-permute-start | bytes 36872 | tf_op jit(solution)/shard_map/ppermute | solution.py:25
  141.1 217.8 %all-reduce.9.cloned.1.call-start = ((), (), s32[]{:S(2)}) async-start(), calls=%async_computation.1 | async-start | bytes 4194304 | tf_op jit(solution)/shard_map/psum | solution.py:221
  297.6 5.2 %collective-permute-start.16 = (bf16[2,3,74,256]{3,2,1,0:T(8,128)(2,1)S(1)}, bf16[2,3,74,256]{3,2,1,0:T(8,128)(2,1)S(1)}, u32[]{:S(2)}, u32[]{:S(2)}) collective-permute-start(bf16[2,3,74,256]{3,2,1,0:T(8,128)(2,1)S(1)} %get-tuple-element.146), channel_id=1, source_target_pairs={{0,32},{32,64},{64,96},{1,33},{33,65},{65,97},{2,34},{34,66},{66,9... | collective-permute-start | bytes 681992 | tf_op jit(solution)/shard_map/ppermute | solution.py:25
  300.2 4.7 %collective-permute-start.17 = (bf16[2,3,74,256]{3,2,1,0:T(8,128)(2,1)S(1)}, bf16[2,3,74,256]{3,2,1,0:T(8,128)(2,1)S(1)}, u32[]{:S(2)}, u32[]{:S(2)}) collective-permute-start(bf16[2,3,74,256]{3,2,1,0:T(8,128)(2,1)S(1)} %get-tuple-element.147), channel_id=1, source_target_pairs={{32,0},{64,32},{96,64},{33,1},{65,33},{97,65},{34,2},{66,34},{98,6... | collective-permute-start | bytes 681992 | tf_op jit(solution)/shard_map/ppermute | solution.py:28
  (140 other events, 715.1 us)
Sparse Core Ops, SparseCore 0:
  141.2 155.0 all-reduce.6
  299.2 59.6 all-reduce.8
